TPU v7x, 32 devices: a whole 2x2x4 slice. The times are simulated.
32 devices in a mesh: prompts: 2 (over y), patch: 4 (over z), cfg: 2 (over core), batch: 2 (over x).
Axes of the slice: x: 2, y: 2, z: 4, core: 2. Of those that a mesh axis runs over, the one named last changes fastest.
Arguments:
- latent: float32 [4, 64, 1280], P(('prompts', 'batch'), 'patch'), parts along dimension 0, may hold values from -16 to 16
- stale_keys: bfloat16 [4, 64, 1280], P('prompts', 'patch', 'batch'), parts along dimension 0, may hold values from -18 to 18
- stale_values: bfloat16 [4, 64, 1280], P('prompts', 'patch', 'batch'), parts along dimension 0, may hold values from -12 to 12
- text_keys: bfloat16 [4, 77, 1280], P(('prompts', 'cfg'), None, 'batch'), parts along dimension 0, may hold values from -160 to 160
- text_values: bfloat16 [4, 77, 1280], P(('prompts', 'cfg'), None, 'batch'), parts along dimension 0, may hold values from -6 to 6
- w_query: bfloat16 [1280, 1280], P(None, 'batch'), may hold values from -0.15625 to 0.15625
- w_key: bfloat16 [1280, 1280], P(None, 'batch'), may hold values from -0.15625 to 0.15625
- w_value: bfloat16 [1280, 1280], P(None, 'batch'), may hold values from -0.15625 to 0.15625
- w_out: bfloat16 [1280, 1280], P('batch'), may hold values from -0.15625 to 0.15625
- norm_gain: float32 [1280], replicated, may hold values from 0.25 to 1.75
- norm_bias: float32 [1280], replicated, may hold values from -0.5 to 0.5
- timesteps: int32 [6], P('prompts'), parts along dimension 0, may hold values from 0 to 999, as said below
Outputs:
- final_latent: float32 [4, 64, 1280], P(('prompts', 'batch'), 'patch'), parts along dimension 0
- final_keys: bfloat16 [4, 64, 1280], P('prompts', 'patch', 'batch'), parts along dimension 0
- final_values: bfloat16 [4, 64, 1280], P('prompts', 'patch', 'batch'), parts along dimension 0
There are 2 independent parts, one for each index of `prompts`. A program takes and returns all parts, laid end to end along the dimension named above; an argument that names none is the same for every part. Nothing has to cross between parts.
Inputs may be any that keep to these rules, and one draw needn't show every extreme that they name: `timesteps`: strictly falling from the first entry to the last.
All inputs are finite; a program needn't handle non-finite values.
Results may differ from a plain program's by a relative error of at most 0.035.
Values may be sent and summed in bfloat16 or wider, within the bound.
No kernel may reach another device: no remote copies, remote signals or barrier semaphores. Data moves between devices by JAX's collectives and lax.ppermute only.
A program may use at most 64 MiB of HBM per device.

v0:
```python
import math
import jax
import jax.numpy as jnp
from jax import lax
from jax.sharding import PartitionSpec as P

HEAD = 64
GROUPS = 32
STEPS = 2
guide_weight = 5.0
norm_eps = 1e-06


def from_partner(shard, axis, stride):
    return lax.ppermute(shard, axis, [(i, i ^ 1 << stride) for i in range(lax.axis_size(axis))])


def alpha_bar(step_index):
    grid = jnp.arange(1000, dtype=jnp.int32)
    ramp = grid.astype(jnp.float32) / 999.0
    root = math.sqrt(0.00085) + ramp * (math.sqrt(0.012) - math.sqrt(0.00085))
    logs = jnp.cumsum(jnp.log1p(-root * root))
    picked = (grid == step_index).astype(jnp.float32)
    return jnp.exp(jnp.sum(picked * logs))


def sampler_weights(now, after):
    a_now = alpha_bar(now)
    a_next = alpha_bar(after)
    keep = jnp.sqrt(a_next / a_now)
    push = jnp.sqrt(1.0 - a_next) - keep * jnp.sqrt(1.0 - a_now)
    return (keep, push)


def split_heads(block):
    return block.reshape(block.shape[0], block.shape[1], block.shape[2] // HEAD, HEAD)


def block_scores(queries, keys):
    return jnp.einsum(
        "bqhd,bkhd->bhqk", queries, keys, preferred_element_type=jnp.float32
    ) * HEAD ** (-0.5)


def body(
    latent,
    stale_keys,
    stale_values,
    text_keys,
    text_values,
    w_query,
    w_key,
    w_value,
    w_out,
    norm_gain,
    norm_bias,
    timesteps,
):
    state = latent[0]
    tok_rows = state.shape[0]
    width = state.shape[1]
    images = stale_keys.shape[0]
    local_width = w_query.shape[1]
    w_joint = jnp.concatenate([w_query, w_key, w_value], axis=1)
    patch_index = lax.axis_index("patch")
    half_index = lax.axis_index("cfg")
    group_width = width // GROUPS
    count = float(tok_rows * lax.axis_size("patch") * group_width)
    text_k = jnp.broadcast_to(text_keys, (images,) + text_keys.shape[1:])
    text_v = jnp.broadcast_to(text_values, (images,) + text_values.shape[1:])
    prior_k, prior_v = (stale_keys, stale_values)
    for step in range(STEPS):
        grouped = state.reshape(tok_rows, GROUPS, group_width)
        sums = jnp.sum(grouped, axis=(0, 2))
        squares = jnp.sum(grouped * grouped, axis=(0, 2))
        sums, squares = lax.psum((sums, squares), "patch")
        mean = sums / count
        scale = lax.rsqrt(squares / count - mean * mean + norm_eps)
        normed = ((grouped - mean[None, :, None]) * scale[None, :, None]).reshape(
            tok_rows, width
        ) * norm_gain + norm_bias
        normed = normed.astype(jnp.bfloat16)[None]
        piece = lax.all_gather(normed, "batch", axis=0, tiled=True)
        flat = piece.reshape(piece.shape[0] * tok_rows, width)
        joint_rows = jnp.dot(flat, w_joint, preferred_element_type=jnp.float32).astype(jnp.bfloat16)
        joint = joint_rows.reshape(piece.shape[0], tok_rows, 3 * local_width)
        queries = split_heads(joint[:, :, :local_width])
        fresh_k = joint[:, :, local_width : 2 * local_width]
        fresh_v = joint[:, :, 2 * local_width :]
        near_k = split_heads(jnp.concatenate([fresh_k, text_k], axis=1))
        near_v = split_heads(jnp.concatenate([fresh_v, text_v], axis=1))
        scores = block_scores(queries, near_k)
        top = jnp.max(scores, axis=-1)
        weights = jnp.exp(scores - top[..., None])
        start_acc = jnp.einsum(
            "bhqk,bkhd->bhqd",
            weights.astype(jnp.bfloat16),
            near_v,
            preferred_element_type=jnp.float32,
        )
        top_old = top
        total_old = jnp.sum(weights, axis=-1)
        piece_k = lax.all_gather(prior_k, "patch", axis=1, tiled=True)
        piece_v = lax.all_gather(prior_v, "patch", axis=1, tiled=True)
        piece_scores = block_scores(queries, split_heads(piece_k))
        place = jnp.arange(piece_k.shape[1], dtype=jnp.int32)
        own_rows = place // tok_rows == patch_index
        piece_scores = jnp.where(own_rows[None, None, None, :], -1e30, piece_scores)
        top_new = jnp.maximum(top_old, jnp.max(piece_scores, axis=-1))
        fade = jnp.exp(top_old - top_new)
        piece_weights = jnp.exp(piece_scores - top_new[..., None])
        total_new = total_old * fade + jnp.sum(piece_weights, axis=-1)
        acc_new = start_acc * fade[..., None] + jnp.einsum(
            "bhqk,bkhd->bhqd",
            piece_weights.astype(jnp.bfloat16),
            split_heads(piece_v),
            preferred_element_type=jnp.float32,
        )
        top = top_new
        attended = jnp.transpose(acc_new / total_new[..., None], (0, 2, 1, 3)).astype(jnp.bfloat16)
        attended = attended.reshape(images, tok_rows, local_width)
        rows_all = attended.reshape(images * tok_rows, local_width)
        mixed = lax.psum_scatter(
            jnp.dot(rows_all, w_out, preferred_element_type=jnp.float32).astype(jnp.bfloat16),
            "batch",
            scatter_dimension=0,
            tiled=True,
        ).astype(jnp.float32)
        branch = state + mixed
        other = from_partner(branch, "cfg", 0)
        leading = half_index == 0
        cond = jnp.where(leading, branch, other)
        uncond = jnp.where(leading, other, branch)
        guess = uncond + guide_weight * (cond - uncond)
        keep, push = sampler_weights(timesteps[step], timesteps[step + 1])
        state = keep * state + push * guess
        prior_k, prior_v = (fresh_k, fresh_v)
    return (state[None], prior_k, prior_v)


def solution(mesh):
    return jax.shard_map(
        body,
        mesh=mesh,
        in_specs=(
            P(("prompts", "batch"), "patch", None),
            P("prompts", "patch", "batch"),
            P("prompts", "patch", "batch"),
            P(("prompts", "cfg"), None, "batch"),
            P(("prompts", "cfg"), None, "batch"),
            P(None, "batch"),
            P(None, "batch"),
            P(None, "batch"),
            P("batch", None),
            P(),
            P(),
            P("prompts"),
        ),
        out_specs=(
            P(("prompts", "batch"), "patch", None),
            P("prompts", "patch", "batch"),
            P("prompts", "patch", "batch"),
        ),
        check_vma=False,
    )
```

profile of v0, /device:TPU:0, one launch (start us, length us, event | category | flops | bytes accessed | tf_op | source)
XLA Modules:
  0.0 153.0 jit_solution(90200097315867511)
XLA Ops:
  7.2 1.1 fusion.36
  8.7 13.5 %all-reduce.2 = (f32[32]{0:T(128)S(1)}, f32[32]{0:T(128)S(1)}) all-reduce(f32[32]{0:T(128)S(1)} %reduce_sum.147, f32[32]{0:T(128)S(1)} %reduce_sum.144), channel_id=1, replica_groups=mesh['prompts'=2,'patch'=4,'cfg'=2,'batch'=2] {'patch'}, use_global_device_ids=true, to_apply=%region_10.11 | all-reduce | flops 64 | bytes 512 | tf_op jit(solution)/shard_map/psum | solution.py:76
  22.6 1.1 add_convert_fusion.1
  23.6 4.7 %all_gather.18 = bf16[2,16,1280]{2,1,0:T(8,128)(2,1)S(1)} all-gather(bf16[1,16,1280]{2,1,0:T(8,128)(2,1)S(1)} %add_convert_fusion.1), channel_id=1, replica_groups=mesh['prompts'=2,'patch'=4,'cfg'=2,'batch'=2] {'batch'}, dimensions={0}, use_global_device_ids=true | all-gather | bytes 122880 | tf_op jit(solution)/shard_map/all_gather | solution.py:83
  28.3 1.6 %constant_dynamic-update-slice_fusion.2 = bf16[1280,1920]{1,0:T(8,128)(2,1)S(1)} fusion(bf16[1280,640]{1,0:T(8,128)(2,1)} %param.17), kind=kLoop, calls=%fused_computation.65 | loop fusion | bytes 3276800
  29.9 0.3 constant_dynamic-update-slice_fusion.1
  30.2 0.3 constant_dynamic-update-slice_fusion
  30.5 2.2 %copy-done.1 = bf16[1280,1920]{1,0:T(8,128)(2,1)} copy-done((bf16[1280,1920]{1,0:T(8,128)(2,1)}, bf16[1280,1920]{1,0:T(8,128)(2,1)S(1)}, u32[]{:S(2)}) %copy-start.1) | copy-done | bytes 4915224
  32.7 0.9 convolution_convert_fusion.3
  33.6 0.2 copy.65
  34.3 13.5 %all_gather.19 = bf16[2,64,640]{2,0,1:T(2,128)(2,1)S(1)} all-gather(bf16[2,16,640]{2,0,1:T(2,128)(2,1)S(1)} %copy.70), channel_id=1, replica_groups=mesh['prompts'=2,'patch'=4,'cfg'=2,'batch'=2] {'patch'}, dimensions={1}, use_global_device_ids=true | all-gather | bytes 204800 | tf_op jit(solution)/shard_map/all_gather | solution.py:103
  47.7 0.3 copy.71
  48.3 0.3 fusion.43
  48.5 0.3 fusion.44
  49.1 0.2 copy.69
  49.5 0.8 copy.74
  50.3 13.5 %all_gather.20 = bf16[2,64,640]{2,0,1:T(2,128)(2,1)S(1)} all-gather(bf16[2,16,640]{2,0,1:T(2,128)(2,1)S(1)} %copy.74), channel_id=1, replica_groups=mesh['prompts'=2,'patch'=4,'cfg'=2,'batch'=2] {'patch'}, dimensions={1}, use_global_device_ids=true | all-gather | bytes 204800 | tf_op jit(solution)/shard_map/all_gather | solution.py:104
  63.8 1.0 copy.75
  65.2 0.3 fusion.7
  65.6 1.3 fusion.8
  67.1 1.0 convolution_convert_fusion.1
  68.2 0.3 reduce-window.9
  68.8 0.6 fusion.42
  69.4 2.5 %select_reduce_fusion.2 = (f32[]{:T(128)}, f32[]{:T(128)}, f32[]{:T(128)}) fusion(f32[1024]{0:T(1024)S(1)} %add_bitcast_fusion.1, s32[]{:T(128)} %bitcast, s32[]{:T(128)} %bitcast.3, s32[]{:T(128)} %bitcast.4), kind=kLoop, calls=%fused_computation.73 | loop fusion | flops 8997 | bytes 4024 | tf_op jit(solution)/shard_map/reduce_sum | solution.py:24
  71.9 4.7 %reduce-scatter.3.cloned.1.call-done = bf16[16,1280]{1,0:T(8,128)(2,1)} async-done(((bf16[32,1280]{1,0:T(8,128)(2,1)}), bf16[16,1280]{1,0:T(8,128)(2,1)}) %reduce-scatter.3.cloned.1.call-update) | async-done | bytes 40976 | tf_op jit(solution)/shard_map/reduce_scatter | solution.py:123
  76.6 0.8 bitcast_add_fusion
  77.5 13.6 %all_gather.22 = bf16[2,64,640]{2,0,1:T(2,128)(2,1)S(1)} all-gather(bf16[2,16,640]{2,0,1:T(2,128)(2,1)S(1)} %copy.91), channel_id=1, replica_groups=mesh['prompts'=2,'patch'=4,'cfg'=2,'batch'=2] {'patch'}, dimensions={1}, use_global_device_ids=true | all-gather | bytes 204800 | tf_op jit(solution)/shard_map/all_gather | solution.py:103
  92.7 0.3 copy.81
  93.0 13.7 %all_gather.23 = bf16[2,64,640]{2,0,1:T(2,128)(2,1)S(1)} all-gather(bf16[2,16,640]{2,0,1:T(2,128)(2,1)S(1)} %copy.92), channel_id=1, replica_groups=mesh['prompts'=2,'patch'=4,'cfg'=2,'batch'=2] {'patch'}, dimensions={1}, use_global_device_ids=true | all-gather | bytes 204800 | tf_op jit(solution)/shard_map/all_gather | solution.py:104
  106.7 1.0 copy.84
  107.6 0.8 fusion.35
  108.9 11.7 %all-reduce.1 = (f32[32]{0:T(128)S(1)}, f32[32]{0:T(128)S(1)}) all-reduce(f32[32]{0:T(128)S(1)} %reduce_sum.157, f32[32]{0:T(128)S(1)} %reduce_sum.154), channel_id=1, replica_groups=mesh['prompts'=2,'patch'=4,'cfg'=2,'batch'=2] {'patch'}, use_global_device_ids=true, to_apply=%region_21.22 | all-reduce | flops 64 | bytes 512 | tf_op jit(solution)/shard_map/psum | solution.py:76
  121.0 4.7 %all-gather = bf16[32,1280]{1,0:T(8,128)(2,1)S(1)} all-gather(bf16[16,1280]{1,0:T(8,128)(2,1)S(1)} %add_convert_fusion), channel_id=2, replica_groups=mesh['prompts'=2,'patch'=4,'cfg'=2,'batch'=2] {'batch'}, dimensions={0}, use_global_device_ids=true | all-gather | bytes 122880 | tf_op jit(solution)/shard_map/all_gather | solution.py:83
  125.7 3.3 %convolution_convert_fusion.2 = bf16[32,1920]{1,0:T(8,128)(2,1)S(1)} fusion(bf16[32,1280]{1,0:T(8,128)(2,1)S(1)} %all-gather, bf16[1280,1920]{1,0:T(8,128)(2,1)} %copy-done.1), kind=kOutput, calls=%fused_computation.2 | convolution fusion | flops 157347840 | bytes 5120000 | tf_op jit(solution)/shard_map/dot_general | solution.py:85
  129.0 0.6 fusion.40
  129.7 0.6 copy-done.5
  130.3 0.2 copy.78
  130.8 0.3 fusion.45
  131.1 0.3 fusion.46
  131.4 0.2 fusion.14
  131.6 1.0 copy.80
  133.1 0.3 fusion.3
  133.4 1.3 fusion.9
  134.9 1.0 convolution_convert_fusion
  135.9 7.5 %reduce-scatter.5.cloned.1.call-done = bf16[16,1280]{1,0:T(8,128)(2,1)} async-done(((bf16[32,1280]{1,0:T(8,128)(2,1)}), bf16[16,1280]{1,0:T(8,128)(2,1)}) %reduce-scatter.5.cloned.1.call-update) | async-done | bytes 40976 | tf_op jit(solution)/shard_map/reduce_scatter | solution.py:123
  143.4 0.8 convert_add_fusion
  145.0 0.5 collective-permute-done.1
  145.5 0.7 add_bitcast_fusion
  (80 shorter events, 4.6 us)
Async XLA Ops:
  7.2 59.9 %copy-start = (bf16[640,1280]{1,0:T(8,128)(2,1)S(1)}, bf16[640,1280]{1,0:T(8,128)(2,1)}, u32[]{:S(2)}) copy-start(bf16[640,1280]{1,0:T(8,128)(2,1)} %param.20) | copy-start | bytes 4915204
  7.2 22.7 %copy-start.2 = (bf16[1280,640]{1,0:T(8,128)(2,1)S(1)}, bf16[1280,640]{1,0:T(8,128)(2,1)}, u32[]{:S(2)}) copy-start(bf16[1280,640]{1,0:T(8,128)(2,1)} %param.18) | copy-start | bytes 4915204
  7.2 69.4 %reduce-scatter.3.cloned.1.call-start = ((), (), s32[]{:S(2)}) async-start(), calls=%async_computation.2 | async-start | bytes 122880 | tf_op jit(solution)/shard_map/reduce_scatter | solution.py:123
  22.5 7.6 %copy-start.3 = (bf16[1280,640]{1,0:T(8,128)(2,1)S(1)}, bf16[1280,640]{1,0:T(8,128)(2,1)}, u32[]{:S(2)}) copy-start(bf16[1280,640]{1,0:T(8,128)(2,1)} %param.19) | copy-start | bytes 4915204
  30.2 3.7 %copy-start.6 = (bf16[1,77,640]{2,1,0:T(8,128)(2,1)S(1)}, bf16[1,77,640]{2,1,0:T(8,128)(2,1)}, u32[]{:S(2)}) copy-start(bf16[1,77,640]{2,1,0:T(8,128)(2,1)} %param.15) | copy-start | bytes 295684
  30.2 4.0 %copy-start.8 = (bf16[2,16,640]{2,1,0:T(8,128)(2,1)S(1)}, bf16[2,16,640]{2,1,0:T(8,128)(2,1)}, u32[]{:S(2)}) copy-start(bf16[2,16,640]{2,1,0:T(8,128)(2,1)} %param.13) | copy-start | bytes 122884
  30.5 2.2 %copy-start.1 = (bf16[1280,1920]{1,0:T(8,128)(2,1)}, bf16[1280,1920]{1,0:T(8,128)(2,1)S(1)}, u32[]{:S(2)}) copy-start(bf16[1280,1920]{1,0:T(8,128)(2,1)S(1)} %constant_dynamic-update-slice_fusion) | copy-start | bytes 14745604
  32.7 16.6 %copy-start.7 = (bf16[1,77,640]{2,1,0:T(8,128)(2,1)S(1)}, bf16[1,77,640]{2,1,0:T(8,128)(2,1)}, u32[]{:S(2)}) copy-start(bf16[1,77,640]{2,1,0:T(8,128)(2,1)} %param.16) | copy-start | bytes 295684
  48.0 20.7 %copy-start.11 = (s32[3]{0:T(128)S(1)}, s32[3]{0:T(128)}, u32[]{:S(2)}) copy-start(s32[3]{0:T(128)} %param.23) | copy-start | bytes 40
  48.0 28.5 %copy-start.4 = (f32[1,16,1280]{2,1,0:T(8,128)S(1)}, f32[1,16,1280]{2,1,0:T(8,128)}, u32[]{:S(2)}) copy-start(f32[1,16,1280]{2,1,0:T(8,128)} %param.12) | copy-start | bytes 245764
  48.8 72.1 %copy-start.9 = (f32[1280]{0:T(1024)S(1)}, f32[1280]{0:T(1024)}, u32[]{:S(2)}) copy-start(f32[1280]{0:T(1024)} %param.22) | copy-start | bytes 15364
  48.8 72.1 %copy-start.10 = (f32[1280]{0:T(1024)S(1)}, f32[1280]{0:T(1024)}, u32[]{:S(2)}) copy-start(f32[1280]{0:T(1024)} %param.21) | copy-start | bytes 15364
  68.1 75.3 %reduce-scatter.5.cloned.1.call-start = ((), (), s32[]{:S(2)}) async-start(), calls=%async_computation.3 | async-start | bytes 122880 | tf_op jit(solution)/shard_map/reduce_scatter | solution.py:123
  77.4 30.3 %collective-permute-start = (f32[16,1280]{1,0:T(8,128)S(1)}, f32[16,1280]{1,0:T(8,128)S(1)}, u32[]{:S(2)}, u32[]{:S(2)}) collective-permute-start(f32[16,1280]{1,0:T(8,128)S(1)} %bitcast_add_fusion), channel_id=1, source_target_pairs={{0,2},{2,0},{1,3},{3,1},{4,6},{6,4},{5,7},{7,5},{8,10},{10,8},{9,1... | collective-permute-start | bytes 245768 | tf_op jit(solution)/shard_map/ppermute | solution.py:15
  129.7 0.6 copy-start.5
  144.2 1.3 collective-permute-start.1
Sparse Core Ops, SparseCore 0:
  68.2 8.3 reduce-scatter.2
  136.1 7.2 reduce-scatter.4
where the time goes:
time: 154 us; the launch traced here: 153 us
  blocking collectives  88.9 us (58%)
  between operations  16.9 us (11%)
  local copies, waits for them, and re-layouts  13.4 us (9%)
  waiting for transfers between devices  12.7 us (8%)
  matrix products  10.7 us (7%)
  other arithmetic  10.2 us (7%)
    all_gather x2, blocking collectives, body(): piece_v = lax.all_gather(prior_v, 'patch', axis=1, tiled=True)  27.2 us
    all_gather x2, blocking collectives, body(): piece_k = lax.all_gather(prior_k, 'patch', axis=1, tiled=True)  27.1 us
    psum x2, blocking collectives, body(): sums, squares = lax.psum((sums, squares), 'patch')  25.2 us
    reduce_scatter x2, waiting for transfers between devices, body(): lax.psum_scatter(jnp.dot(rows_all, w_out, preferred_element_type=jnp.floa...  12.1 us
    all_gather x2, blocking collectives, body(): piece = lax.all_gather(normed, 'batch', axis=0, tiled=True)  9.34 us
    unnamed x30, local copies, waits for them, and re-layouts  5.64 us
    dot_general x2, matrix products, body(): jnp.dot(flat, w_joint, preferred_element_type=jnp.float32)  4.26 us
  transfers between devices with their start and end apart: 4, of which 3 were waited for; matrix products, arithmetic and copies ran while one was open for 3% of the time, Pallas kernels for 0%

commit v1 on v0

--- a/solution.py
+++ b/solution.py
@@ -80,7 +80,19 @@
             tok_rows, width
         ) * norm_gain + norm_bias
         normed = normed.astype(jnp.bfloat16)[None]
-        piece = lax.all_gather(normed, "batch", axis=0, tiled=True)
+
+        def attach_face(in_array):
+            return jnp.concatenate(
+                jax.lax.all_to_all(
+                    jnp.stack([in_array for _ in range(jax.lax.axis_size("batch"))], axis=0),
+                    "batch",
+                    0,
+                    0,
+                ),
+                axis=0,
+            )
+
+        piece = attach_face(normed)
         flat = piece.reshape(piece.shape[0] * tok_rows, width)
         joint_rows = jnp.dot(flat, w_joint, preferred_element_type=jnp.float32).astype(jnp.bfloat16)
         joint = joint_rows.reshape(piece.shape[0], tok_rows, 3 * local_width)

time: 154 us -> 165 us (1.071)
  blocking collectives: 88.9 us -> 79.6 us
  starting transfers between devices: 0.22 us -> 6.86 us
  local copies, waits for them, and re-layouts: 13.4 us -> 18.7 us
  waiting for transfers between devices: 12.7 us -> 17.6 us
  matrix products: 10.7 us -> 13 us
    all_gather x2 -> x0, blocking collectives: 9.34 us -> none  [body(): piece = lax.all_gather(normed, 'batch', axis=0, tiled=True)]
    all_to_all x0 -> x2, starting transfers between devices: none -> 6.64 us  [attach_face(): jax.lax.all_to_all(jnp.stack([in_array for _ in range(jax.lax.axis_size('...]
    reduce_scatter x2, waiting for transfers between devices: 12.1 us -> 17.1 us  [body(): lax.psum_scatter(jnp.dot(rows_all, w_out, preferred_element_type=jnp.floa...]
    concatenate x1, local copies, waits for them, and re-layouts: 0.28 us -> 2.85 us  [body(): w_joint = jnp.concatenate([w_query, w_key, w_value], axis=1)]
    dot_general x2, matrix products: 4.26 us -> 6.66 us  [body(): jnp.dot(flat, w_joint, preferred_element_type=jnp.float32)]
    unnamed x30 -> x28, local copies, waits for them, and re-layouts: 5.64 us -> 6.59 us
  transfers between devices with their start and end apart: 4 -> 6, of which waited for: 3 -> 3; matrix products, arithmetic and copies ran while one was open for 3% -> 12% of each run, Pallas kernels for 0% -> 0%
where the time goes in v1:
time: 165 us; the launch traced here: 164 us
  blocking collectives  79.6 us (48%)
  local copies, waits for them, and re-layouts  18.7 us (11%)
  waiting for transfers between devices  17.6 us (11%)
  between operations  16.8 us (10%)
  matrix products  13 us (8%)
  other arithmetic  11.4 us (7%)
  starting transfers between devices  6.86 us (4%)
    all_gather x2, blocking collectives, body(): piece_v = lax.all_gather(prior_v, 'patch', axis=1, tiled=True)  27.1 us
    all_gather x2, blocking collectives, body(): piece_k = lax.all_gather(prior_k, 'patch', axis=1, tiled=True)  27.1 us
    psum x2, blocking collectives, body(): sums, squares = lax.psum((sums, squares), 'patch')  25.4 us
    reduce_scatter x2, waiting for transfers between devices, body(): lax.psum_scatter(jnp.dot(rows_all, w_out, preferred_element_type=jnp.floa...  17.1 us
    dot_general x2, matrix products, body(): jnp.dot(flat, w_joint, preferred_element_type=jnp.float32)  6.66 us
    all_to_all x2, starting transfers between devices, attach_face(): jax.lax.all_to_all(jnp.stack([in_array for _ in range(jax.lax.axis_size('...  6.64 us
    unnamed x28, local copies, waits for them, and re-layouts  6.59 us
  transfers between devices with their start and end apart: 6, of which 3 were waited for; matrix products, arithmetic and copies ran while one was open for 12% of the time, Pallas kernels for 0%

profile of v1, /device:TPU:0, one launch (start us, length us, event | category | flops | bytes accessed | tf_op | source)
XLA Modules:
  0.0 164.2 jit_solution(17580894439408109156)
XLA Ops:
  7.2 1.1 fusion.41
  8.7 13.5 %all-reduce.2 = (f32[32]{0:T(128)S(1)}, f32[32]{0:T(128)S(1)}) all-reduce(f32[32]{0:T(128)S(1)} %reduce_sum.147, f32[32]{0:T(128)S(1)} %reduce_sum.144), channel_id=1, replica_groups=mesh['prompts'=2,'patch'=4,'cfg'=2,'batch'=2] {'patch'}, use_global_device_ids=true, to_apply=%region_10.11 | all-reduce | flops 64 | bytes 512 | tf_op jit(solution)/shard_map/psum | solution.py:76
  22.5 0.9 fusion.25
  23.4 0.6 pad_maximum_fusion.4
  24.1 3.3 %all-to-all-start = ((bf16[2,1,16,1280]{3,2,1,0:T(8,128)(2,1)}), bf16[2,1,16,1280]{3,2,1,0:T(8,128)(2,1)S(1)}, u32[]{:S(2)}, u32[]{:S(2)}) async-start(bf16[2,1,16,1280]{3,2,1,0:T(8,128)(2,1)} %pad_maximum_fusion.4), calls=%async_computation | async-start | bytes 163840 | tf_op jit(solution)/shard_map/all_to_all | solution.py:86
  27.5 2.9 %constant_dynamic-update-slice_fusion.2 = bf16[1280,1920]{1,0:T(8,128)(2,1)} fusion(bf16[1280,640]{1,0:T(8,128)(2,1)} %param.17), kind=kLoop, calls=%fused_computation.72 | loop fusion | bytes 3276800
  30.3 1.7 %copy.64 = bf16[77,640]{0,1:T(8,128)(2,1)} copy(bf16[77,640]{1,0:T(8,128)(2,1)} %bitcast.119) | data formatting | bytes 197120 | tf_op jit(solution)/shard_map/broadcast_in_dim | solution.py:69
  32.0 0.8 copy.70
  32.8 13.5 %all_gather.12 = bf16[2,64,640]{2,0,1:T(2,128)(2,1)S(1)} all-gather(bf16[2,16,640]{2,0,1:T(2,128)(2,1)S(1)} %copy.70), channel_id=1, replica_groups=mesh['prompts'=2,'patch'=4,'cfg'=2,'batch'=2] {'patch'}, dimensions={1}, use_global_device_ids=true | all-gather | bytes 204800 | tf_op jit(solution)/shard_map/all_gather | solution.py:115
  46.3 1.0 copy.71
  47.3 1.1 copy.68
  48.3 1.4 copy.74
  49.8 0.3 reduce-window.9
  50.3 1.4 constant_dynamic-update-slice_fusion.1
  51.7 2.9 %constant_dynamic-update-slice_fusion = bf16[1280,1920]{1,0:T(8,128)(2,1)} fusion(bf16[1280,1920]{1,0:T(8,128)(2,1)} %constant_dynamic-update-slice_fusion.1, bf16[1280,640]{1,0:T(8,128)(2,1)} %param.19), kind=kLoop, calls=%fused_computation.70 | loop fusion | bytes 3276800 | tf_op jit(solution)/shard_map/concatenate | solution.py:64
  54.5 13.6 %all_gather.13 = bf16[2,64,640]{2,0,1:T(2,128)(2,1)S(1)} all-gather(bf16[2,16,640]{2,0,1:T(2,128)(2,1)S(1)} %copy-done.5), channel_id=1, replica_groups=mesh['prompts'=2,'patch'=4,'cfg'=2,'batch'=2] {'patch'}, dimensions={1}, use_global_device_ids=true | all-gather | bytes 204800 | tf_op jit(solution)/shard_map/all_gather | solution.py:116
  68.1 0.9 copy.75
  69.1 3.3 %convolution_convert_fusion.3 = bf16[32,1920]{1,0:T(8,128)(2,1)S(1)} fusion(bf16[32,1280]{1,0:T(8,128)(2,1)S(1)} %bitcast.117, bf16[1280,1920]{1,0:T(8,128)(2,1)} %constant_dynamic-update-slice_fusion), kind=kOutput, calls=%fused_computation.3 | convolution fusion | flops 157347840 | bytes 5120000 | tf_op jit(solution)/shard_map/dot_general | solution.py:97
  72.5 0.2 copy.65
  73.1 0.3 fusion.48
  73.4 0.3 fusion.49
  74.6 0.3 fusion.7
  74.9 1.3 fusion.8
  76.5 1.0 convolution_convert_fusion.1
  77.5 0.7 fusion.47
  78.2 8.2 %reduce-scatter.3.cloned.1.call-done = bf16[16,1280]{1,0:T(8,128)(2,1)} async-done(((bf16[32,1280]{1,0:T(8,128)(2,1)}), bf16[16,1280]{1,0:T(8,128)(2,1)}) %reduce-scatter.3.cloned.1.call-update) | async-done | bytes 40976 | tf_op jit(solution)/shard_map/reduce_scatter | solution.py:135
  86.4 0.8 bitcast_add_fusion
  87.3 2.6 %select_reduce_fusion.2 = (f32[]{:T(128)}, f32[]{:T(128)}, f32[]{:T(128)}) fusion(f32[1024]{0:T(1024)S(1)} %add_bitcast_fusion.1, s32[]{:T(128)} %bitcast, s32[]{:T(128)} %bitcast.3, s32[]{:T(128)} %bitcast.4), kind=kLoop, calls=%fused_computation.80 | loop fusion | flops 8997 | bytes 4024 | tf_op jit(solution)/shard_map/reduce_sum | solution.py:24
  91.4 13.6 %all_gather.14 = bf16[2,64,640]{2,0,1:T(2,128)(2,1)S(1)} all-gather(bf16[2,16,640]{2,0,1:T(2,128)(2,1)S(1)} %copy.91), channel_id=1, replica_groups=mesh['prompts'=2,'patch'=4,'cfg'=2,'batch'=2] {'patch'}, dimensions={1}, use_global_device_ids=true | all-gather | bytes 204800 | tf_op jit(solution)/shard_map/all_gather | solution.py:115
  105.0 0.3 copy.81
  105.3 0.8 fusion.40
  106.5 12.0 %all-reduce.1 = (f32[32]{0:T(128)S(1)}, f32[32]{0:T(128)S(1)}) all-reduce(f32[32]{0:T(128)S(1)} %reduce_sum.157, f32[32]{0:T(128)S(1)} %reduce_sum.154), channel_id=1, replica_groups=mesh['prompts'=2,'patch'=4,'cfg'=2,'batch'=2] {'patch'}, use_global_device_ids=true, to_apply=%region_21.22 | all-reduce | flops 64 | bytes 512 | tf_op jit(solution)/shard_map/psum | solution.py:76
  118.9 0.6 pad_maximum_fusion.5
  119.5 3.3 %all-to-all-start.1 = ((bf16[2,1,16,1280]{3,2,1,0:T(8,128)(2,1)}), bf16[2,1,16,1280]{3,2,1,0:T(8,128)(2,1)S(1)}, u32[]{:S(2)}, u32[]{:S(2)}) async-start(bf16[2,1,16,1280]{3,2,1,0:T(8,128)(2,1)} %pad_maximum_fusion.5), calls=%async_computation.2 | async-start | bytes 163840 | tf_op jit(solution)/shard_map/all_to_all | solution.py:86
  122.9 13.5 %all_gather.15 = bf16[2,64,640]{2,0,1:T(2,128)(2,1)S(1)} all-gather(bf16[2,16,640]{2,0,1:T(2,128)(2,1)S(1)} %copy.92), channel_id=1, replica_groups=mesh['prompts'=2,'patch'=4,'cfg'=2,'batch'=2] {'patch'}, dimensions={1}, use_global_device_ids=true | all-gather | bytes 204800 | tf_op jit(solution)/shard_map/all_gather | solution.py:116
  136.4 1.0 copy.84
  137.4 3.3 %convolution_convert_fusion.2 = bf16[32,1920]{1,0:T(8,128)(2,1)S(1)} fusion(bf16[32,1280]{1,0:T(8,128)(2,1)S(1)} %bitcast.118, bf16[1280,1920]{1,0:T(8,128)(2,1)} %constant_dynamic-update-slice_fusion), kind=kOutput, calls=%fused_computation.2 | convolution fusion | flops 157347840 | bytes 5120000 | tf_op jit(solution)/shard_map/dot_general | solution.py:97
  140.7 0.2 copy.78
  141.3 0.3 fusion.50
  141.6 0.3 fusion.51
  142.1 0.2 copy.80
  142.8 0.3 fusion.3
  143.1 1.3 fusion.9
  144.6 1.0 convolution_convert_fusion
  145.6 8.9 %reduce-scatter.5.cloned.1.call-done = bf16[16,1280]{1,0:T(8,128)(2,1)} async-done(((bf16[32,1280]{1,0:T(8,128)(2,1)}), bf16[16,1280]{1,0:T(8,128)(2,1)}) %reduce-scatter.5.cloned.1.call-update) | async-done | bytes 40976 | tf_op jit(solution)/shard_map/reduce_scatter | solution.py:135
  154.5 0.8 convert_add_fusion
  156.2 0.5 collective-permute-done.1
  156.6 0.7 add_bitcast_fusion
  (82 shorter events, 4.7 us)
Async XLA Ops:
  7.2 69.3 %copy-start = (bf16[640,1280]{1,0:T(8,128)(2,1)S(1)}, bf16[640,1280]{1,0:T(8,128)(2,1)}, u32[]{:S(2)}) copy-start(bf16[640,1280]{1,0:T(8,128)(2,1)} %param.20) | copy-start | bytes 4915204
  7.2 43.1 %copy-start.1 = (bf16[1280,640]{1,0:T(8,128)(2,1)S(1)}, bf16[1280,640]{1,0:T(8,128)(2,1)}, u32[]{:S(2)}) copy-start(bf16[1280,640]{1,0:T(8,128)(2,1)} %param.18) | copy-start | bytes 4915204
  24.1 45.0 %all-to-all-start = ((bf16[2,1,16,1280]{3,2,1,0:T(8,128)(2,1)}), bf16[2,1,16,1280]{3,2,1,0:T(8,128)(2,1)S(1)}, u32[]{:S(2)}, u32[]{:S(2)}) async-start(bf16[2,1,16,1280]{3,2,1,0:T(8,128)(2,1)} %pad_maximum_fusion.4), calls=%async_computation | async-start | bytes 163840 | tf_op jit(solution)/shard_map/all_to_all | solution.py:86
  27.4 59.0 %reduce-scatter.3.cloned.1.call-start = ((), (), s32[]{:S(2)}) async-start(), calls=%async_computation.4 | async-start | bytes 122880 | tf_op jit(solution)/shard_map/reduce_scatter | solution.py:135
  50.2 4.3 %copy-start.5 = (bf16[2,16,640]{2,0,1:T(2,128)(2,1)S(1)}, bf16[2,16,640]{2,0,1:T(2,128)(2,1)}, u32[]{:S(2)}) copy-start(bf16[2,16,640]{2,0,1:T(2,128)(2,1)} %copy.74) | copy-start | bytes 122884
  51.6 21.2 %copy-start.4 = (bf16[77,640]{0,1:T(8,128)(2,1)S(1)}, bf16[77,640]{0,1:T(8,128)(2,1)}, u32[]{:S(2)}) copy-start(bf16[77,640]{0,1:T(8,128)(2,1)} %copy.64) | copy-start | bytes 295684
  54.5 18.9 %copy-start.3 = (bf16[2,64,640]{1,2,0:T(8,128)(2,1)S(1)}, bf16[2,64,640]{1,2,0:T(8,128)(2,1)}, u32[]{:S(2)}) copy-start(bf16[2,64,640]{1,2,0:T(8,128)(2,1)} %copy.71) | copy-start | bytes 491524
  72.4 5.1 %copy-start.10 = (s32[3]{0:T(128)S(1)}, s32[3]{0:T(128)}, u32[]{:S(2)}) copy-start(s32[3]{0:T(128)} %param.23) | copy-start | bytes 40
  72.4 14.0 %copy-start.2 = (f32[1,16,1280]{2,1,0:T(8,128)S(1)}, f32[1,16,1280]{2,1,0:T(8,128)}, u32[]{:S(2)}) copy-start(f32[1,16,1280]{2,1,0:T(8,128)} %param.12) | copy-start | bytes 245764
  72.9 46.0 %copy-start.8 = (f32[1280]{0:T(1024)S(1)}, f32[1280]{0:T(1024)}, u32[]{:S(2)}) copy-start(f32[1280]{0:T(1024)} %param.22) | copy-start | bytes 15364
  72.9 46.0 %copy-start.9 = (f32[1280]{0:T(1024)S(1)}, f32[1280]{0:T(1024)}, u32[]{:S(2)}) copy-start(f32[1280]{0:T(1024)} %param.21) | copy-start | bytes 15364
  87.2 18.1 %collective-permute-start = (f32[16,1280]{1,0:T(8,128)S(1)}, f32[16,1280]{1,0:T(8,128)S(1)}, u32[]{:S(2)}, u32[]{:S(2)}) collective-permute-start(f32[16,1280]{1,0:T(8,128)S(1)} %bitcast_add_fusion), channel_id=1, source_target_pairs={{0,2},{2,0},{1,3},{3,1},{4,6},{6,4},{5,7},{7,5},{8,10},{10,8},{9,1... | collective-permute-start | bytes 245768 | tf_op jit(solution)/shard_map/ppermute | solution.py:15
  119.5 17.8 %all-to-all-start.1 = ((bf16[2,1,16,1280]{3,2,1,0:T(8,128)(2,1)}), bf16[2,1,16,1280]{3,2,1,0:T(8,128)(2,1)S(1)}, u32[]{:S(2)}, u32[]{:S(2)}) async-start(bf16[2,1,16,1280]{3,2,1,0:T(8,128)(2,1)} %pad_maximum_fusion.5), calls=%async_computation.2 | async-start | bytes 163840 | tf_op jit(solution)/shard_map/all_to_all | solution.py:86
  122.9 31.7 %reduce-scatter.5.cloned.1.call-start = ((), (), s32[]{:S(2)}) async-start(), calls=%async_computation.5 | async-start | bytes 122880 | tf_op jit(solution)/shard_map/reduce_scatter | solution.py:135
  140.7 16.6 %copy-start.6 = (bf16[2,16,640]{2,1,0:T(8,128)(2,1)}, bf16[2,16,640]{2,1,0:T(8,128)(2,1)S(1)}, u32[]{:S(2)}) copy-start(bf16[2,16,640]{2,1,0:T(8,128)(2,1)S(1)} %get-tuple-element.20) | copy-start | bytes 122884
  140.7 16.6 %copy-start.7 = (bf16[2,16,640]{2,1,0:T(8,128)(2,1)}, bf16[2,16,640]{2,1,0:T(8,128)(2,1)S(1)}, u32[]{:S(2)}) copy-start(bf16[2,16,640]{2,1,0:T(8,128)(2,1)S(1)} %get-tuple-element.21) | copy-start | bytes 122884
  155.3 1.3 collective-permute-start.1
Sparse Core Ops, SparseCore 0:
  77.6 8.7 reduce-scatter.2
  145.8 8.7 reduce-scatter.4
